TPU v7x, 512 devices: a whole 4x4x16 slice. The times are simulated.
512 devices in a mesh: walk: 64 (over z, y), col: 8 (over x, core).
Axes of the slice: x: 4, y: 4, z: 16, core: 2. Of those that a mesh axis runs over, the one named last changes fastest.
Arguments:
- jacobian: float32 [384, 524288], P('walk', 'col'), may hold values from -25 to 25
- prev_update: float32 [8, 65536], P('col', 'walk'), may hold values from -6 to 6
- base_energy: float32 [384], P('walk'), may hold values from -6 to 6
- elec_pos: float32 [384, 3, 66], P('walk'), may hold values from -8 to 8
- atom_pos: float32 [3, 21], replicated, may hold values from -6 to 6
- quad_ratio: float32 [384, 21, 66, 12], P('walk'), may hold values from -1.2 to 1.2
- rotation: int32 [384, 66], P('walk'), may hold values from 0 to 15
- channels: int32 [21], replicated, may hold values from 1 to 3
- ecp_coef: float32 [21, 3], replicated, may hold values from 0.5 to 2
- ecp_expo: float32 [21, 3], replicated, may hold values from 0.2 to 2
Outputs:
- local_energy: float32 [384], P('walk')
- update: float32 [8, 65536], P('col', 'walk')
All inputs are finite; a program needn't handle non-finite values.
Results may differ from a plain program's by a relative error of at most 0.0003.
Values sent between devices are 32-bit elements; how exact they have to be, the bound alone decides.
No kernel may reach another device: no remote copies, remote signals or barrier semaphores. Data moves between devices by JAX's collectives and lax.ppermute only.
A program may use at most 64 MiB of HBM per device.

v0:
```python
import math
import jax
import jax.numpy as jnp
from jax import lax
from jax.sharding import PartitionSpec as P

NROT = 16
momentum = 0.9
damping = 0.1


def icosa_points():
    golden = (1.0 + math.sqrt(5.0)) / 2.0
    length = math.sqrt(1.0 + golden * golden)
    rows = []
    for first in (-1.0, 1.0):
        for second in (-golden, golden):
            rows.append((0.0, first / length, second / length))
            rows.append((first / length, second / length, 0.0))
            rows.append((second / length, 0.0, first / length))
    return jnp.asarray(rows, dtype=jnp.float32).T


def rotation_table(count):
    angle = jnp.arange(count, dtype=jnp.float32)
    turn_z = 2.0 * math.pi * angle / count
    turn_x = 0.9 * angle
    cz, sz = (jnp.cos(turn_z), jnp.sin(turn_z))
    cx, sx = (jnp.cos(turn_x), jnp.sin(turn_x))
    zeros = jnp.zeros_like(cz)
    matrix = jnp.stack(
        [
            jnp.stack([cz, -sz * cx, sz * sx], axis=-1),
            jnp.stack([sz, cz * cx, -cz * sx], axis=-1),
            jnp.stack([zeros, sx, cx], axis=-1),
        ],
        axis=1,
    )
    points = icosa_points()
    rotated = matrix[:, :, 0, None] * points[None, 0, :]
    rotated = rotated + matrix[:, :, 1, None] * points[None, 1, :]
    rotated = rotated + matrix[:, :, 2, None] * points[None, 2, :]
    return rotated.reshape(count, -1)


def nonlocal_energy(elec_pos, atom_pos, quad_ratio, rotation, channels, ecp_coef, ecp_expo):
    walkers, electrons = rotation.shape
    count = NROT
    table = rotation_table(count)
    onehot = (rotation[:, :, None] == jnp.arange(count, dtype=jnp.int32)[None, None, :]).astype(
        jnp.float32
    )
    rotated = jnp.einsum("wek,kf->wef", onehot, table, precision=lax.Precision.HIGHEST)
    rotated = rotated.reshape(walkers, electrons, 3, -1)
    diff = elec_pos[:, :, None, :] - atom_pos[None, :, :, None]
    dist2 = jnp.sum(diff * diff, axis=1)
    unit = diff / jnp.sqrt(dist2 + 0.01)[:, None, :, :]
    cosang = unit[:, 0, :, :, None] * rotated[:, None, :, 0, :]
    cosang = cosang + unit[:, 1, :, :, None] * rotated[:, None, :, 1, :]
    cosang = cosang + unit[:, 2, :, :, None] * rotated[:, None, :, 2, :]
    quad = quad_ratio.shape[-1]
    lmax = ecp_coef.shape[1]
    lower = jnp.ones_like(cosang)
    upper = cosang
    total = jnp.zeros((walkers,), jnp.float32)
    for level in range(lmax):
        if level == 0:
            poly = lower
        elif level == 1:
            poly = upper
        else:
            fresh = ((2 * level - 1) * cosang * upper - (level - 1) * lower) / level
            lower, upper = (upper, fresh)
            poly = fresh
        angular = jnp.sum(poly * quad_ratio, axis=-1) / quad
        active = (channels > level).astype(jnp.float32)
        radial = ecp_coef[None, :, level, None] * jnp.exp(-ecp_expo[None, :, level, None] * dist2)
        term = (2 * level + 1) * active[None, :, None] * radial * angular
        total = total + jnp.sum(term, axis=(1, 2))
    return total


def sum_pieces(first, second):
    first_sum, second_sum = lax.psum((first, second), ("walk", "col"))
    return (first_sum, second_sum)


def body(
    jacobian,
    prev_update,
    base_energy,
    elec_pos,
    atom_pos,
    quad_ratio,
    rotation,
    channels,
    ecp_coef,
    ecp_expo,
):
    energy_mine = base_energy + nonlocal_energy(
        elec_pos, atom_pos, quad_ratio, rotation, channels, ecp_coef, ecp_expo
    )
    columns = lax.all_to_all(jacobian, "walk", split_axis=1, concat_axis=0, tiled=True)
    walkers = columns.shape[0]
    params_total = columns.shape[1] * lax.axis_size("walk") * lax.axis_size("col")
    scale = 1.0 / params_total
    centred = columns - jnp.mean(columns, axis=0, keepdims=True)
    prev_mine = prev_update[0]
    gram_part = (
        jnp.dot(
            centred, centred.T, precision=lax.Precision.HIGHEST, preferred_element_type=jnp.float32
        )
        * scale
    )
    along_part = (
        jnp.dot(
            centred, prev_mine, precision=lax.Precision.HIGHEST, preferred_element_type=jnp.float32
        )
        * scale
    )
    extra = along_part[:, None]
    gram, extra_sum = sum_pieces(gram_part, extra)
    along = extra_sum[:, 0]
    energies = lax.all_gather(energy_mine, "walk", axis=0, tiled=True)
    eps = -(energies - jnp.mean(energies)) / math.sqrt(walkers)
    system = gram + damping * jnp.eye(walkers, dtype=jnp.float32)
    factor = jnp.linalg.cholesky(system)
    solved = jax.scipy.linalg.cho_solve((factor, True), eps - momentum * along)
    update_mine = (
        jnp.dot(
            solved, centred, precision=lax.Precision.HIGHEST, preferred_element_type=jnp.float32
        )
        + momentum * prev_mine
    )
    return (energy_mine, update_mine[None, :])


def solution(mesh):
    in_specs = (
        P("walk", "col"),
        P("col", "walk"),
        P("walk"),
        P("walk", None, None),
        P(),
        P("walk", None, None, None),
        P("walk", None),
        P(),
        P(),
        P(),
    )
    out_specs = (P("walk"), P("col", "walk"))
    return jax.shard_map(body, mesh=mesh, in_specs=in_specs, out_specs=out_specs, check_vma=False)
```

profile of v0, /device:TPU:1, one launch (start us, length us, event | category | flops | bytes accessed | tf_op | source)
XLA Modules:
  0.0 826.4 jit_solution(6028116304954348564)
XLA Ops:
  7.3 19.4 %all-to-all-start = ((f32[6,64,1024]{2,0,1:T(8,128)}), f32[6,64,1024]{2,0,1:T(8,128)S(1)}, u32[]{:S(2)}, u32[]{:S(2)}) async-start(f32[6,64,1024]{2,0,1:T(8,128)} %bitcast.162), calls=%async_computation | async-start | bytes 4194304 | tf_op jit(solution)/shard_map/all_to_all | solution.py:103
  28.4 1.3 dynamic-slice.3
  30.9 0.6 multiply_reduce_fusion
  31.8 0.5 fusion.57
  32.3 187.9 %all-reduce.1 = f32[384]{0:T(512)S(1)} all-reduce(f32[384]{0:T(512)S(1)} %get-tuple-element.32), channel_id=1, replica_groups=mesh['walk'=64,'col'=8] {'walk'}, use_global_device_ids=true, to_apply=%add.1 | all-reduce | flops 384 | bytes 3072
  220.3 0.6 reduce_sum.89
  221.7 1.6 subtract_bitcast_fusion
  223.3 1.6 sub.49
  225.0 3.4 convolution_multiply_fusion
  228.4 1.4 convolution_reduce_fusion
  229.9 133.3 %psum.15 = f32[384,1]{0,1:T(1,128)S(1)} all-reduce(f32[384,1]{0,1:T(1,128)S(1)} %broadcast_in_dim.6), channel_id=1, replica_groups=mesh['walk'=64,'col'=8] {'walk','col'}, use_global_device_ids=true, to_apply=%region_16.17 | all-reduce | flops 384 | bytes 3072 | tf_op jit(solution)/shard_map/psum | solution.py:84
  363.3 355.0 %all-reduce.4.cloned.1.call-done = f32[384,384]{0,1:T(8,128)} async-done(((f32[384,384]{0,1:T(8,128)}), f32[384,384]{0,1:T(8,128)}) %all-reduce.4.cloned.1.call-update) | async-done | bytes 589840 | tf_op jit(solution)/shard_map/psum | solution.py:84
  718.2 1.2 select_add_fusion
  719.8 11.7 %cholesky.76 = f32[128,128]{1,0:T(8,128)S(1)} custom-call(f32[128,128]{1,0:T(8,128)S(1)} %cholesky.189), custom_call_target="Cholesky" | custom-call | tf_op jit(solution)/shard_map/jit(cholesky)/cholesky | solution.py:127
  731.5 9.8 %custom-call.26 = f32[1,128,128]{1,2,0:T(8,128)S(1)} custom-call(f32[1,128,128]{2,1,0:T(8,128)S(1)} %get-tuple-element.45), custom_call_target="InvertDiagBlocksLowerTriangular" | custom-call | tf_op jit(solution)/shard_map/jit(cholesky)/cholesky | solution.py:127
  742.1 11.7 %cholesky.160 = f32[128,128]{1,0:T(8,128)S(1)} custom-call(f32[128,128]{1,0:T(8,128)S(1)} %cholesky.193), custom_call_target="Cholesky" | custom-call | tf_op jit(solution)/shard_map/jit(cholesky)/cholesky | solution.py:127
  754.0 10.0 %custom-call.27 = f32[1,128,128]{1,2,0:T(8,128)S(1)} custom-call(f32[1,128,128]{2,1,0:T(8,128)S(1)} %get-tuple-element.43), custom_call_target="InvertDiagBlocksLowerTriangular" | custom-call | tf_op jit(solution)/shard_map/jit(cholesky)/cholesky | solution.py:127
  764.0 0.3 convolution_dynamic-update-slice_fusion
  764.3 0.4 convolution_subtract_fusion.1
  764.7 11.7 %cholesky.179 = f32[128,128]{1,0:T(8,128)S(1)} custom-call(f32[128,128]{1,0:T(8,128)S(1)} %convolution_subtract_fusion.1), custom_call_target="Cholesky" | custom-call | tf_op jit(solution)/shard_map/jit(cholesky)/cholesky | solution.py:127
  776.6 0.7 compare_reduce_fusion
  777.3 0.6 compare_reduce_fusion.1
  779.9 6.7 while.1
  780.0 0.6 fusion.71
  780.6 1.4 dynamic-slice.8
  782.2 0.6 fusion.71
  782.8 1.4 dynamic-slice.8
  784.4 0.6 fusion.71
  785.0 1.4 dynamic-slice.8
  786.6 29.5 %custom-call.28 = f32[3,128,128]{1,2,0:T(8,128)S(1)} custom-call(f32[3,128,128]{2,1,0:T(8,128)S(1)} %get-tuple-element.9), custom_call_target="InvertDiagBlocksLowerTriangular" | custom-call | tf_op jit(solution)/shard_map/jit(_cho_solve)/triangular_solve | solution.py:128
  818.0 0.9 fusion.33
  818.9 0.6 multiply_add_fusion.1
  (115 shorter events, 6.6 us)
Async XLA Ops:
  7.2 20.8 %copy-start.11 = (f32[12]{0:T(128)S(1)}, f32[12]{0:T(128)}, u32[]{:S(2)}) copy-start(f32[12]{0:T(128)} %constant.198) | copy-start | bytes 148
  7.2 20.9 %copy-start.10 = (f32[12]{0:T(128)S(1)}, f32[12]{0:T(128)}, u32[]{:S(2)}) copy-start(f32[12]{0:T(128)} %constant.200) | copy-start | bytes 148
  7.2 20.9 %copy-start.9 = (f32[12]{0:T(128)S(1)}, f32[12]{0:T(128)}, u32[]{:S(2)}) copy-start(f32[12]{0:T(128)} %constant.202) | copy-start | bytes 148
  7.2 21.2 %copy-start.3 = (f32[6,3,66]{2,1,0:T(4,128)S(1)}, f32[6,3,66]{2,1,0:T(4,128)}, u32[]{:S(2)}) copy-start(f32[6,3,66]{2,1,0:T(4,128)} %param.14) | copy-start | bytes 14260
  7.2 23.1 %copy-start.4 = (f32[3,21]{1,0:T(4,128)S(1)}, f32[3,21]{1,0:T(4,128)}, u32[]{:S(2)}) copy-start(f32[3,21]{1,0:T(4,128)} %param.15) | copy-start | bytes 760
  7.2 23.2 %copy-start.12 = (s32[21]{0:T(128)S(1)}, s32[21]{0:T(128)}, u32[]{:S(2)}) copy-start(s32[21]{0:T(128)} %param.18) | copy-start | bytes 256
  7.2 23.3 %copy-start.6 = (f32[21,3]{0,1:T(4,128)S(1)}, f32[21,3]{0,1:T(4,128)}, u32[]{:S(2)}) copy-start(f32[21,3]{0,1:T(4,128)} %param.20) | copy-start | bytes 760
  7.2 23.3 %copy-start.7 = (f32[21,3]{0,1:T(4,128)S(1)}, f32[21,3]{0,1:T(4,128)}, u32[]{:S(2)}) copy-start(f32[21,3]{0,1:T(4,128)} %param.19) | copy-start | bytes 760
  7.3 23.3 %copy-start.5 = (s32[6,66]{1,0:T(8,128)S(1)}, s32[6,66]{1,0:T(8,128)}, u32[]{:S(2)}) copy-start(s32[6,66]{1,0:T(8,128)} %param.17) | copy-start | bytes 4756
  7.3 214.3 %all-to-all-start = ((f32[6,64,1024]{2,0,1:T(8,128)}), f32[6,64,1024]{2,0,1:T(8,128)S(1)}, u32[]{:S(2)}, u32[]{:S(2)}) async-start(f32[6,64,1024]{2,0,1:T(8,128)} %bitcast.162), calls=%async_computation | async-start | bytes 4194304 | tf_op jit(solution)/shard_map/all_to_all | solution.py:103
  26.7 4.2 copy-start.1
  26.7 691.5 %all-reduce.4.cloned.1.call-start = ((), (), s32[]{:S(2)}) async-start(), calls=%async_computation.1 | async-start | bytes 1179648 | tf_op jit(solution)/shard_map/psum | solution.py:84
  30.5 1.2 copy-start.8
  225.0 3.5 copy-start.2
  718.2 1.4 copy-start
Sparse Core Ops, SparseCore 0:
  228.5 489.6 all-reduce.3
where the time goes:
time: 827 us; the launch traced here: 826 us
  waiting for transfers between devices  355 us (43%)
  blocking collectives  321 us (39%)
  other arithmetic  92.2 us (11%)
  starting transfers between devices  19.5 us (2%)
  between operations  17.8 us (2%)
  local copies, waits for them, and re-layouts  11.5 us (1%)
  matrix products  9.1 us (1%)
    psum x1, waiting for transfers between devices, sum_pieces(): first_sum, second_sum = lax.psum((first, second), ('walk', 'col'))  355 us
    unnamed x1, blocking collectives  188 us
    psum x1, blocking collectives, sum_pieces(): first_sum, second_sum = lax.psum((first, second), ('walk', 'col'))  133 us
    another operation x10, other arithmetic, body(): factor = jnp.linalg.cholesky(system)  56.4 us
    another operation x3, other arithmetic, body(): solved = jax.scipy.linalg.cho_solve((factor, True), eps - momentum * along)  29.5 us
    all_to_all x1, starting transfers between devices, body(): lax.all_to_all(jacobian, 'walk', split_axis=1, concat_axis=0, tiled=True)  19.4 us
  transfers between devices with their start and end apart: 2, of which 1 were waited for; matrix products, arithmetic and copies ran while one was open for 1% of the time, Pallas kernels for 0%

commit v1 on v0

--- a/solution.py
+++ b/solution.py
@@ -81,7 +81,7 @@
 
 
 def sum_pieces(first, second):
-    first_sum, second_sum = lax.psum((first, second), ("walk", "col"))
+    first_sum, second_sum = lax.psum(lax.psum((first, second), "walk"), "col")
     return (first_sum, second_sum)
 
 

time: 827 us -> 576 us (0.70)
  blocking collectives: 321 us -> 158 us
  waiting for transfers between devices: 355 us -> 264 us
    unnamed x1 -> x0, blocking collectives: 188 us -> none
    psum x1 -> x2, waiting for transfers between devices: 355 us -> 174 us  [sum_pieces(): first_sum, second_sum = lax.psum(lax.psum((first, second), 'walk'), 'col')]
    all_to_all x1, waiting for transfers between devices: 0.01 us -> 89.8 us  [body(): lax.all_to_all(jacobian, 'walk', split_axis=1, concat_axis=0, tiled=True)]
    psum x1 -> x2, blocking collectives: 133 us -> 158 us  [sum_pieces(): first_sum, second_sum = lax.psum(lax.psum((first, second), 'walk'), 'col')]
  transfers between devices with their start and end apart: 2 -> 3, of which waited for: 1 -> 3; matrix products, arithmetic and copies ran while one was open for 1% -> 1% of each run, Pallas kernels for 0% -> 0%
where the time goes in v1:
time: 576 us; the launch traced here: 575 us
  waiting for transfers between devices  264 us (46%)
  blocking collectives  158 us (27%)
  other arithmetic  93 us (16%)
  starting transfers between devices  19.5 us (3%)
  between operations  17.8 us (3%)
  local copies, waits for them, and re-layouts  13.3 us (2%)
  matrix products  9.1 us (2%)
    psum x2, waiting for transfers between devices, sum_pieces(): first_sum, second_sum = lax.psum(lax.psum((first, second), 'walk'), 'col')  174 us
    psum x2, blocking collectives, sum_pieces(): first_sum, second_sum = lax.psum(lax.psum((first, second), 'walk'), 'col')  158 us
    all_to_all x1, waiting for transfers between devices, body(): lax.all_to_all(jacobian, 'walk', split_axis=1, concat_axis=0, tiled=True)  89.8 us
    another operation x10, other arithmetic, body(): factor = jnp.linalg.cholesky(system)  56.4 us
    another operation x3, other arithmetic, body(): solved = jax.scipy.linalg.cho_solve((factor, True), eps - momentum * along)  30.4 us
    all_to_all x1, starting transfers between devices, body(): lax.all_to_all(jacobian, 'walk', split_axis=1, concat_axis=0, tiled=True)  19.4 us
  transfers between devices with their start and end apart: 3, of which 3 were waited for; matrix products, arithmetic and copies ran while one was open for 1% of the time, Pallas kernels for 0%

profile of v1, /device:TPU:1, one launch (start us, length us, event | category | flops | bytes accessed | tf_op | source)
XLA Modules:
  0.0 574.7 jit_solution(9547280777765200089)
XLA Ops:
  7.3 19.4 %all-to-all-start = ((f32[6,64,1024]{2,0,1:T(8,128)}), f32[6,64,1024]{2,0,1:T(8,128)S(1)}, u32[]{:S(2)}, u32[]{:S(2)}) async-start(f32[6,64,1024]{2,0,1:T(8,128)} %bitcast.162), calls=%async_computation | async-start | bytes 4194304 | tf_op jit(solution)/shard_map/all_to_all | solution.py:103
  28.4 1.3 dynamic-slice.3
  31.8 89.8 %all-to-all-done = f32[6,64,1024]{2,0,1:T(8,128)S(1)} async-done(((f32[6,64,1024]{2,0,1:T(8,128)}), f32[6,64,1024]{2,0,1:T(8,128)S(1)}, u32[]{:S(2)}, u32[]{:S(2)}) %all-to-all-start) | async-done | bytes 1572896 | tf_op jit(solution)/shard_map/all_to_all | solution.py:103
  121.7 1.6 subtract_bitcast_fusion
  123.3 1.6 sub.49
  125.0 3.4 convolution_multiply_fusion
  129.1 1.4 convolution_reduce_fusion
  130.5 113.8 %all-reduce.2 = (f32[384,1]{0,1:T(1,128)S(1)}, f32[384]{0:T(512)S(1)}) all-reduce(f32[384,1]{0,1:T(1,128)S(1)} %broadcast_in_dim.6, f32[384]{0:T(512)S(1)} %get-tuple-element.34), channel_id=1, replica_groups=mesh['walk'=64,'col'=8] {'walk'}, use_global_device_ids=true, to_apply=%region_17.18 | all-reduce | flops 768 | bytes 6144 | tf_op jit(solution)/shard_map/psum | solution.py:84
  244.3 0.6 reduce_sum.89
  245.5 44.0 %psum.31 = f32[384,1]{0,1:T(1,128)S(1)} all-reduce(f32[384,1]{0,1:T(1,128)S(1)} %get-tuple-element.32), channel_id=1, replica_groups=mesh['walk'=64,'col'=8] {'col'}, use_global_device_ids=true, to_apply=%region_18.19 | all-reduce | flops 384 | bytes 3072 | tf_op jit(solution)/shard_map/psum | solution.py:84
  289.5 92.3 %all-reduce.6.cloned.1.call-done = f32[384,384]{0,1:T(8,128)} async-done(((f32[384,384]{0,1:T(8,128)}), f32[384,384]{0,1:T(8,128)}) %all-reduce.6.cloned.1.call-update) | async-done | bytes 589840 | tf_op jit(solution)/shard_map/psum | solution.py:84
  381.9 82.1 %all-reduce.8.cloned.1.call-done = f32[384,384]{0,1:T(8,128)} async-done(((f32[384,384]{0,1:T(8,128)}), f32[384,384]{0,1:T(8,128)}) %all-reduce.8.cloned.1.call-update) | async-done | bytes 589840 | tf_op jit(solution)/shard_map/psum | solution.py:84
  464.0 1.2 select_add_fusion
  465.5 11.7 %cholesky.76 = f32[128,128]{1,0:T(8,128)S(1)} custom-call(f32[128,128]{1,0:T(8,128)S(1)} %cholesky.189), custom_call_target="Cholesky" | custom-call | tf_op jit(solution)/shard_map/jit(cholesky)/cholesky | solution.py:127
  477.3 9.8 %custom-call.26 = f32[1,128,128]{1,2,0:T(8,128)S(1)} custom-call(f32[1,128,128]{2,1,0:T(8,128)S(1)} %get-tuple-element.47), custom_call_target="InvertDiagBlocksLowerTriangular" | custom-call | tf_op jit(solution)/shard_map/jit(cholesky)/cholesky | solution.py:127
  487.9 11.7 %cholesky.160 = f32[128,128]{1,0:T(8,128)S(1)} custom-call(f32[128,128]{1,0:T(8,128)S(1)} %cholesky.193), custom_call_target="Cholesky" | custom-call | tf_op jit(solution)/shard_map/jit(cholesky)/cholesky | solution.py:127
  499.8 10.0 %custom-call.27 = f32[1,128,128]{1,2,0:T(8,128)S(1)} custom-call(f32[1,128,128]{2,1,0:T(8,128)S(1)} %get-tuple-element.45), custom_call_target="InvertDiagBlocksLowerTriangular" | custom-call | tf_op jit(solution)/shard_map/jit(cholesky)/cholesky | solution.py:127
  510.5 11.7 %cholesky.179 = f32[128,128]{1,0:T(8,128)S(1)} custom-call(f32[128,128]{1,0:T(8,128)S(1)} %convolution_subtract_fusion.1), custom_call_target="Cholesky" | custom-call | tf_op jit(solution)/shard_map/jit(cholesky)/cholesky | solution.py:127
  522.3 0.7 compare_reduce_fusion
  523.1 0.6 compare_reduce_fusion.1
  525.7 8.5 %while.1 = (s32[]{:T(128)}, f32[384,384]{0,1:T(8,128)S(1)}, s32[3,2]{0,1:T(2,128)S(1)}, f32[3,128,128]{2,1,0:T(8,128)}, s32[]{:T(128)}) while((s32[]{:T(128)}, f32[384,384]{0,1:T(8,128)S(1)}, s32[3,2]{0,1:T(2,128)S(1)}, f32[3,128,128]{2,1,0:T(8,128)}, s32[]{:T(128)}) %tuple.50), condition=%wide.while_cond, body=%wide.while_body.sunk | while | flops 2 | bytes 393829 | solution.py:128
  525.8 0.6 fusion.71
  526.3 1.4 dynamic-slice.8
  527.9 0.6 bitcast_dynamic-update-slice_fusion.2
  528.6 0.6 fusion.71
  529.2 1.4 dynamic-slice.8
  530.7 0.6 bitcast_dynamic-update-slice_fusion.2
  532.0 1.4 dynamic-slice.8
  533.5 0.6 bitcast_dynamic-update-slice_fusion.2
  534.1 30.3 %custom-call.28 = f32[3,128,128]{1,2,0:T(8,128)S(1)} custom-call(f32[3,128,128]{2,1,0:T(8,128)} %get-tuple-element.9), custom_call_target="InvertDiagBlocksLowerTriangular" | custom-call | tf_op jit(solution)/shard_map/jit(_cho_solve)/triangular_solve | solution.py:128
  566.4 0.9 fusion.33
  567.3 0.6 multiply_add_fusion.1
  (118 shorter events, 8.9 us)
Async XLA Ops:
  7.2 20.8 %copy-start.11 = (f32[12]{0:T(128)S(1)}, f32[12]{0:T(128)}, u32[]{:S(2)}) copy-start(f32[12]{0:T(128)} %constant.198) | copy-start | bytes 148
  7.2 20.9 %copy-start.10 = (f32[12]{0:T(128)S(1)}, f32[12]{0:T(128)}, u32[]{:S(2)}) copy-start(f32[12]{0:T(128)} %constant.200) | copy-start | bytes 148
  7.2 20.9 %copy-start.9 = (f32[12]{0:T(128)S(1)}, f32[12]{0:T(128)}, u32[]{:S(2)}) copy-start(f32[12]{0:T(128)} %constant.202) | copy-start | bytes 148
  7.2 21.2 %copy-start.3 = (f32[6,3,66]{2,1,0:T(4,128)S(1)}, f32[6,3,66]{2,1,0:T(4,128)}, u32[]{:S(2)}) copy-start(f32[6,3,66]{2,1,0:T(4,128)} %param.14) | copy-start | bytes 14260
  7.2 23.1 %copy-start.4 = (f32[3,21]{1,0:T(4,128)S(1)}, f32[3,21]{1,0:T(4,128)}, u32[]{:S(2)}) copy-start(f32[3,21]{1,0:T(4,128)} %param.15) | copy-start | bytes 760
  7.2 23.2 %copy-start.12 = (s32[21]{0:T(128)S(1)}, s32[21]{0:T(128)}, u32[]{:S(2)}) copy-start(s32[21]{0:T(128)} %param.18) | copy-start | bytes 256
  7.2 23.3 %copy-start.6 = (f32[21,3]{0,1:T(4,128)S(1)}, f32[21,3]{0,1:T(4,128)}, u32[]{:S(2)}) copy-start(f32[21,3]{0,1:T(4,128)} %param.20) | copy-start | bytes 760
  7.2 23.3 %copy-start.7 = (f32[21,3]{0,1:T(4,128)S(1)}, f32[21,3]{0,1:T(4,128)}, u32[]{:S(2)}) copy-start(f32[21,3]{0,1:T(4,128)} %param.19) | copy-start | bytes 760
  7.3 23.3 %copy-start.5 = (s32[6,66]{1,0:T(8,128)S(1)}, s32[6,66]{1,0:T(8,128)}, u32[]{:S(2)}) copy-start(s32[6,66]{1,0:T(8,128)} %param.17) | copy-start | bytes 4756
  7.3 114.3 %all-to-all-start = ((f32[6,64,1024]{2,0,1:T(8,128)}), f32[6,64,1024]{2,0,1:T(8,128)S(1)}, u32[]{:S(2)}, u32[]{:S(2)}) async-start(f32[6,64,1024]{2,0,1:T(8,128)} %bitcast.162), calls=%async_computation | async-start | bytes 4194304 | tf_op jit(solution)/shard_map/all_to_all | solution.py:103
  26.7 4.2 copy-start.1
  26.7 355.1 %all-reduce.6.cloned.1.call-start = ((), (), s32[]{:S(2)}) async-start(), calls=%async_computation.1 | async-start | bytes 1179648 | tf_op jit(solution)/shard_map/psum | solution.py:84
  125.0 3.5 copy-start.8
  125.0 4.1 copy-start.2
  128.4 335.6 %all-reduce.8.cloned.1.call-start = ((), (), s32[]{:S(2)}) async-start(), calls=%async_computation.2 | async-start | bytes 1179648 | tf_op jit(solution)/shard_map/psum | solution.py:84
  464.0 1.4 copy-start
Sparse Core Ops, SparseCore 0:
  128.6 253.2 all-reduce.5
  384.3 79.6 all-reduce.7
